TPU v7x, 128 devices: a whole 4x4x4 slice. The times are simulated.
128 devices in a mesh: gx: 8 (over x, core), gy: 16 (over z, y).
Axes of the slice: x: 4, y: 4, z: 4, core: 2. Of those that a mesh axis runs over, the one named last changes fastest.
Arguments:
- table: bfloat16 [65536, 512], P('gy'), may hold values from -40 to 40
- history: bfloat16 [2, 128, 1024, 512], P(None, 'gy', 'gx'), may hold values from -40 to 40
- lengths: int32 [16, 8], P('gy'), may hold values from 341 to 1024, as said below
- assignment: int32 [16, 8], P('gy'), may hold values from 0 to 7, each once within a row
- cand_owner: int32 [196608, 1], P(('gx', 'gy')), may hold values from 0 to 15; in each aligned block of 1536 rows (0 to 1535, 1536 to 3071, ...) at most 192 rows name the same one
- cand_row: int32 [196608], P(('gx', 'gy')), may hold values from 0 to 4095
- norm_gain: float32 [2, 512], replicated, may hold values from 0.1 to 1.9
- w_query: bfloat16 [2, 512, 1024], replicated, may hold values from -0.5 to 0.5
- w_key: bfloat16 [2, 512, 1024], replicated, may hold values from -1 to 1
- attn_gain: float32 [2, 512], replicated, may hold values from 0.1 to 1.9
- w_out: bfloat16 [2, 512, 512], replicated, may hold values from -0.25 to 0.25
Outputs:
- cand_out: bfloat16 [196608, 512], P(('gx', 'gy'))
Inputs may be any that keep to these rules, and one draw needn't show every extreme that they name: `lengths`: some user has exactly 1024 live positions and some exactly 341. `assignment`: each row names each of its column's 8 users once. `cand_owner`: within the 1536 candidates of one device no table shard is named more than 192 times.
All inputs are finite; a program needn't handle non-finite values.
Results may differ from a plain program's by a relative error of at most 0.0075.
Values may be sent and summed in bfloat16 or wider, within the bound.
A program may use at most 128 MiB of HBM per device.

v0:
```python
import jax
import jax.numpy as jnp
from jax import lax
from jax.sharding import Mesh
from jax.sharding import PartitionSpec as P

HEADS = 4
LAYERS = 2
GX = ("gx_0", "gx_1")
GX_GY = ("gx_0", "gx_1", "gy")


epsilon = 1e-06


def split_up(array, dim, size):
    dims = array.shape
    tiles = array.reshape(*dims[:dim], size, dims[dim] // size, *dims[dim + 1 :])
    return jnp.moveaxis(tiles, dim, 0)


def laid_out(tiles, dim):
    dims = list(tiles.shape[1:])
    dims[dim] *= tiles.shape[0]
    return jnp.moveaxis(tiles, 0, dim).reshape(dims)


def moved_by_axis(tiles, axes, turns):
    dims = [lax.axis_size(a) for a in axes]
    tiles = tiles.reshape(*dims, *tiles.shape[1:])
    for k in turns:
        tiles = lax.all_to_all(tiles, axes[k], split_axis=k, concat_axis=k, tiled=True)
    return tiles.reshape(-1, *tiles.shape[len(axes) :])


def two_step_exchange(array, groups, turns, split_dim, concat_dim):
    size = lax.axis_size(groups[0]) * lax.axis_size(groups[1])
    tiles = split_up(array, split_dim, size)
    return laid_out(moved_by_axis(tiles, groups, turns), concat_dim)


def rms_scale(vector, gain_row):
    return (
        vector * lax.rsqrt(jnp.mean(vector * vector, axis=-1, keepdims=True) + epsilon) * gain_row
    )


def project_history(states, gain_row, weight):
    normed = rms_scale(states.astype(jnp.float32), gain_row).astype(jnp.bfloat16)
    return jax.nn.silu(jnp.dot(normed, weight, preferred_element_type=jnp.float32)).astype(
        jnp.bfloat16
    )


def attend(query_part, key_rows, value_rows, live_mask):
    count_rows = query_part.shape[0]
    count_keys = key_rows.shape[0]
    head_size = query_part.shape[1] // HEADS
    queries = query_part.reshape(count_rows, HEADS, head_size)
    keyed = key_rows.reshape(count_keys, HEADS, head_size)
    valued = value_rows.reshape(count_keys, HEADS, head_size)
    scores = jnp.einsum(
        "chd,lhd->hcl", queries, keyed, preferred_element_type=jnp.float32
    ) * head_size ** (-0.5)
    weights = jnp.where(live_mask[None, None, :], jax.nn.silu(scores), 0.0).astype(jnp.bfloat16)
    attended = jnp.einsum("hcl,lhd->chd", weights, valued, preferred_element_type=jnp.float32)
    return attended.reshape(count_rows, HEADS * head_size)


def local(
    table,
    history,
    lengths,
    assignment,
    cand_owner,
    cand_row,
    norm_gain,
    w_query,
    w_key,
    attn_gain,
    w_out,
):
    groups = lax.axis_size("gy")
    members = lax.axis_size(GX)
    cand_count = cand_row.shape[0]
    feature_count = table.shape[1]
    capacity = 2 * cand_count // groups
    owners = cand_owner[:, 0]
    onehot = (owners[:, None] == jnp.arange(groups, dtype=jnp.int32)[None, :]).astype(jnp.int32)
    prior_count = jnp.cumsum(onehot, axis=0) - onehot
    flat_slot = owners * capacity + jnp.sum(prior_count * onehot, axis=1)
    requests = (
        jnp.zeros((groups * capacity,), jnp.int32)
        .at[flat_slot]
        .set(cand_row)
        .reshape(groups, capacity)
    )
    fetched_rows = jnp.take(
        table, lax.all_to_all(requests, "gy", split_axis=0, concat_axis=0, tiled=True), axis=0
    )
    returned = lax.all_to_all(fetched_rows, "gy", split_axis=0, concat_axis=0, tiled=True)
    stream = jnp.take(returned.reshape(groups * capacity, feature_count), flat_slot, axis=0).astype(
        jnp.float32
    )
    own_index = lax.axis_index(GX)
    member_ids = jnp.arange(members, dtype=jnp.int32)
    user_order = assignment[0]
    slot_index = jnp.sum(jnp.where(member_ids == own_index, user_order, 0))
    length = jnp.sum(jnp.where(member_ids == slot_index, lengths[0], 0))
    ordered = jnp.take(history, user_order, axis=1)
    span = history.shape[2]
    total_span = span * members
    live_mask = jnp.arange(total_span, dtype=jnp.int32) < length
    arrived_all = two_step_exchange(ordered, ("gx_0", "gx_1"), (1, 0), 1, 2)
    for layer_index in range(LAYERS):
        gain_row = norm_gain[layer_index]
        normed = rms_scale(stream, gain_row).astype(jnp.bfloat16)
        gate_query = jax.nn.silu(
            jnp.dot(normed, w_query[layer_index], preferred_element_type=jnp.float32)
        ).astype(jnp.bfloat16)
        key_value = project_history(arrived_all[layer_index, 0], gain_row, w_key[layer_index])
        attended = attend(
            gate_query[:, feature_count:],
            key_value[:, :feature_count],
            key_value[:, feature_count:],
            live_mask,
        )
        gated_out = (
            rms_scale(attended, attn_gain[layer_index])
            * gate_query[:, :feature_count].astype(jnp.float32)
        ).astype(jnp.bfloat16)
        stream = stream + jnp.dot(gated_out, w_out[layer_index], preferred_element_type=jnp.float32)
    return stream.astype(jnp.bfloat16)


def solution(mesh):
    finer = Mesh(mesh.devices.reshape(4, 2, mesh.shape["gy"]), ("gx_0", "gx_1", "gy"))
    return jax.shard_map(
        local,
        mesh=finer,
        in_specs=(
            P("gy", None),
            P(None, "gy", GX, None),
            P("gy", None),
            P("gy", None),
            P(GX_GY, None),
            P(GX_GY),
            P(),
            P(),
            P(),
            P(),
            P(),
        ),
        out_specs=P(GX_GY, None),
        check_vma=False,
    )
```

profile of v0, /device:TPU:0, one launch (start us, length us, event | category | flops | bytes accessed | tf_op | source)
XLA Modules:
  0.0 178.8 jit_solution(4860279381990146323)
XLA Ops:
  0.0 0.0 copy-start
  0.0 0.8 fusion.47
  0.8 0.7 compare_and_fusion.1
  1.5 0.1 copy-done
  1.6 2.0 %gather_fusion.2 = bf16[8,2,128,512]{3,2,1,0:T(8,128)(2,1)} fusion(bf16[2,8,128,512]{3,2,1,0:T(8,128)(2,1)S(1)} %copy-done, s32[1024]{0:T(1024)S(1)} %pad_clamp_fusion.1), kind=kCustom, calls=%fused_computation.2 | custom fusion | bytes 4194336 | tf_op jit(solution)/shard_map/jit(_take)/gather | solution.py:110
  3.6 1.9 %bitcast_select_fusion = bf16[2,8,1,128,512]{4,3,0,1,2:T(8,128)(2,1)S(1)} fusion(bf16[8,2,128,512]{3,2,1,0:T(8,128)(2,1)} %gather_fusion.2, pred[8]{0:T(512)(128)(4,1)S(1)} %compare_and_fusion.1), kind=kLoop, calls=%fused_computation.45 | loop fusion | flops 1048576 | bytes 4194312 | tf_op jit(solution)/shard_map/jit(_take)/select_n | solution.py:110
  5.5 1.5 copy.35
  7.0 3.9 %all-to-all-start.2 = ((bf16[4,2,2,1,128,512]{5,4,2,0,3,1:T(8,128)(2,1)}), bf16[4,2,2,1,128,512]{5,4,2,0,3,1:T(8,128)(2,1)S(1)}, u32[]{:S(2)}, u32[]{:S(2)}) async-start(bf16[4,2,2,1,128,512]{5,4,2,0,3,1:T(8,128)(2,1)} %copy.35), calls=%async_computation.2 | async-start | bytes 4194304 | tf_op jit(solution)/shard_map/all_to_all | solution.py:32
  10.9 0.0 copy-done.8
  11.0 4.5 %reduce-window.6 = s32[16,12,128]{2,1,0:T(8,128)S(1)} reduce-window(s32[16,12,128]{2,1,0:T(8,128)S(1)} %fusion.38, s32[]{:T(128)} %constant.76.clone.1), window={size=1x1x128 pad=0_0x0_0x127_0}, to_apply=%region_0.0 | reduce-window | flops 3121152 | bytes 196612 | tf_op jit(solution)/shard_map/reduce-window
  15.6 0.4 slice_reduce_fusion
  16.0 0.2 reduce-window.9
  16.2 0.1 broadcast_add_fusion
  16.3 0.1 fusion.41
  16.4 6.4 %scatter_custom_fusion = s32[3072]{0:T(1024)S(1)} fusion(s32[1536]{0:T(1024)S(1)} %reduce.8, s32[1536]{0:T(1024)} %param.16, s32[]{:T(128)} %constant.76.clone.1), kind=kCustom, calls=%fused_computation.85 | custom fusion | bytes 12800 | tf_op jit(solution)/shard_map/scatter | solution.py:95
  22.8 0.7 all_to_all.19
  23.5 0.0 all-to-all-done.2
  23.5 8.2 %all-to-all-start = ((s32[16,1,192]{2,1,0:T(1,128)}), s32[16,1,192]{2,1,0:T(1,128)S(1)}, u32[]{:S(2)}, u32[]{:S(2)}) async-start(s32[16,1,192]{2,1,0:T(1,128)} %all_to_all.19), calls=%async_computation | async-start | bytes 32768 | tf_op jit(solution)/shard_map/all_to_all | solution.py:99
  31.6 0.7 fusion.45
  32.3 1.5 copy.36
  33.9 5.3 %all-to-all-done = s32[16,1,192]{2,1,0:T(1,128)S(1)} async-done(((s32[16,1,192]{2,1,0:T(1,128)}), s32[16,1,192]{2,1,0:T(1,128)S(1)}, u32[]{:S(2)}, u32[]{:S(2)}) %all-to-all-start) | async-done | bytes 12320 | tf_op jit(solution)/shard_map/all_to_all | solution.py:99
  39.2 4.3 %all-to-all-start.3 = ((bf16[4,2,2,1,128,512]{5,4,2,1,3,0:T(8,128)(2,1)}), bf16[4,2,2,1,128,512]{5,4,2,1,3,0:T(8,128)(2,1)S(1)}, u32[]{:S(2)}, u32[]{:S(2)}) async-start(bf16[4,2,2,1,128,512]{5,4,2,1,3,0:T(8,128)(2,1)} %copy.36), calls=%async_computation.3 | async-start | bytes 4194304 | tf_op jit(solution)/shard_map/all_to_all | solution.py:32
  43.5 1.3 fusion.46
  44.8 0.0 copy-done.10
  44.9 0.6 fusion.57
  45.4 0.1 fusion.42
  45.5 0.1 reshape.238
  45.6 16.0 %gather_fusion = bf16[3072,512]{1,0:T(8,128)(2,1)} fusion(bf16[4096,512]{1,0:T(8,128)(2,1)} %param.11, s32[3072]{0:T(1024)S(1)} %broadcast_clamp_fusion), kind=kCustom, calls=%fused_computation | custom fusion | bytes 6303744 | tf_op jit(solution)/shard_map/jit(_take)/gather | solution.py:98
  61.6 3.4 %broadcast_select_fusion = bf16[16,192,512]{2,1,0:T(8,128)(2,1)} fusion(bf16[16,192,512]{2,1,0:T(8,128)(2,1)} %bitcast.116, pred[16,192]{1,0:T(8,128)(4,1)S(1)} %compare_and_fusion), kind=kLoop, calls=%fused_computation.31 | loop fusion | flops 1572864 | bytes 6294528 | tf_op jit(solution)/shard_map/jit(_take)/select_n | solution.py:98
  65.0 4.1 %all-to-all-done.3 = bf16[4,2,2,1,128,512]{5,4,2,1,3,0:T(8,128)(2,1)S(1)} async-done(((bf16[4,2,2,1,128,512]{5,4,2,1,3,0:T(8,128)(2,1)}), bf16[4,2,2,1,128,512]{5,4,2,1,3,0:T(8,128)(2,1)S(1)}, u32[]{:S(2)}, u32[]{:S(2)}) %all-to-all-start.3) | async-done | bytes 2097184 | tf_op jit(solution)/shard_map/all_to_all | solution.py:32
  69.0 4.7 %all-to-all-start.1 = ((bf16[16,192,512]{2,1,0:T(8,128)(2,1)}), bf16[16,192,512]{2,1,0:T(8,128)(2,1)}, u32[]{:S(2)}, u32[]{:S(2)}) async-start(bf16[16,192,512]{2,1,0:T(8,128)(2,1)} %broadcast_select_fusion), calls=%async_computation.1 | async-start | bytes 6291456 | tf_op jit(solution)/shard_map/all_to_all | solution.py:101
  73.7 0.7 iota_compare_fusion.2
  74.4 0.0 copy-start.12
  74.4 0.5 fusion.17
  74.9 0.6 fusion.19
  75.5 0.5 copy-done.12
  76.0 1.9 %multiply_convert_fusion.3 = bf16[1024,1024]{0,1:T(8,128)(2,1)S(1)} fusion(bf16[1024,512]{1,0:T(8,128)(2,1)S(1)} %bitcast.121, bf16[2,512,1024]{2,1,0:T(8,128)(2,1)S(1)} %copy-done.12), kind=kOutput, calls=%fused_computation.12 | convolution fusion | flops 1078984704 | bytes 4194304 | tf_op jit(solution)/shard_map/dot_general | solution.py:50
  77.8 1.5 fusion.56
  79.4 1.9 %multiply_convert_fusion.2 = bf16[1024,1024]{0,1:T(8,128)(2,1)S(1)} fusion(bf16[1024,512]{1,0:T(8,128)(2,1)S(1)} %bitcast.120, bf16[2,512,1024]{2,1,0:T(8,128)(2,1)S(1)} %copy-done.12), kind=kOutput, calls=%fused_computation.11 | convolution fusion | flops 1078984704 | bytes 4194304 | tf_op jit(solution)/shard_map/dot_general | solution.py:50
  81.2 1.1 fusion.55
  82.4 33.8 %all-to-all-done.1 = bf16[16,192,512]{2,1,0:T(8,128)(2,1)} async-done(((bf16[16,192,512]{2,1,0:T(8,128)(2,1)}), bf16[16,192,512]{2,1,0:T(8,128)(2,1)}, u32[]{:S(2)}, u32[]{:S(2)}) %all-to-all-start.1) | async-done | bytes 3145760 | tf_op jit(solution)/shard_map/all_to_all | solution.py:101
  116.1 7.8 %gather_fusion.1 = bf16[1536,512]{1,0:T(8,128)(2,1)} fusion(bf16[3072,512]{1,0:T(8,128)(2,1)} %bitcast.3, s32[2048]{0:T(1024)S(1)} %pad_clamp_fusion), kind=kCustom, calls=%fused_computation.1 | custom fusion | bytes 3151872 | tf_op jit(solution)/shard_map/jit(_take)/gather | solution.py:102
  123.9 1.7 copy.34
  125.6 0.4 fusion
  126.1 4.1 %multiply_convert_fusion.1 = bf16[1536,1024]{0,1:T(8,128)(2,1)S(1)} fusion(f32[512]{0:T(512)S(1)} %bitcast.132, f32[1536]{0:T(1024)S(1)} %add_rsqrt_fusion.3, bf16[1536,512]{0,1:T(8,128)(2,1)S(1)} %copy.34, pred[1536]{0:T(1024)(128)(4,1)S(1)} %get-tuple-element.7, bf16[2,512,1024]{2,1,0:T(8,128)(2,1)} %param.18), kind=kOutput, calls=%fused_computation.7 | convolution fusion | flops 1622409216 | bytes 5776896 | tf_op jit(solution)/shard_map/dot_general | solution.py:119
  130.2 1.7 copy-done.3
  131.9 1.2 slice.100
  133.1 14.1 %fusion.10 = (f32[1536]{0:T(1024)S(1)}, f32[4,128,1536]{2,1,0:T(8,128)}) fusion(bf16[1024,4,128]{0,2,1:T(8,128)(2,1)} %bitcast.125, bf16[1536,4,128]{0,2,1:T(8,128)(2,1)} %bitcast.119, bf16[1024,4,128]{0,2,1:T(8,128)(2,1)} %bitcast.124, pred[1024]{0:T(1024)(128)(4,1)S(1)} %iota_compare_fusion.2), kind=kOutput, calls=%fused_computation.28 | convolution fusion | flops 3266836992 | bytes 6822912 | tf_op jit(solution)/shard_map/hcl,lhd->chd/dot_general | solution.py:66
  147.2 3.0 %fusion.8 = bf16[1536,512]{0,1:T(8,128)(2,1)S(1)} fusion(f32[4,128,1536]{2,1,0:T(8,128)} %get-tuple-element.20, bf16[1536,1024]{0,1:T(8,128)(2,1)} %copy-done.3, f32[512]{0:T(512)S(1)} %bitcast.134, f32[1536]{0:T(1024)S(1)} %add_rsqrt_fusion.2), kind=kLoop, calls=%fused_computation.24 | loop fusion | flops 3932160 | bytes 6299648 | tf_op jit(solution)/shard_map/convert_element_type | solution.py:131
  150.2 0.0 copy-start.13
  150.2 1.1 multiply_reduce_fusion
  151.4 0.0 copy-start.4
  151.4 0.4 copy-done.13
  151.8 2.8 %multiply_convert_fusion = bf16[1536,1024]{0,1:T(8,128)(2,1)S(1)} fusion(f32[1536,512]{0,1:T(8,128)S(1)} %get-tuple-element.22, f32[512]{0:T(512)S(1)} %bitcast.130, f32[1536]{0:T(1024)S(1)} %add_rsqrt_fusion.1, bf16[2,512,1024]{2,1,0:T(8,128)(2,1)S(1)} %copy-done.13), kind=kOutput, calls=%fused_computation.6 | convolution fusion | flops 1620836352 | bytes 7350272 | tf_op jit(solution)/shard_map/dot_general | solution.py:119
  154.6 1.7 copy-done.2
  156.3 0.1 slice.105
  156.4 14.0 %fusion.9 = (f32[1536]{0:T(1024)S(1)}, f32[4,128,1536]{2,1,0:T(8,128)}) fusion(bf16[1024,4,128]{0,2,1:T(8,128)(2,1)} %bitcast.123, bf16[1536,4,128]{0,2,1:T(8,128)(2,1)S(1)} %bitcast.118, bf16[1024,4,128]{0,2,1:T(8,128)(2,1)S(1)} %bitcast.122, pred[1024]{0:T(1024)(128)(4,1)S(1)} %iota_compare_fusion.2), kind=kOutput, calls=%fused_computation.26 | convolution fusion | flops 3266836992 | bytes 6822912 | tf_op jit(solution)/shard_map/hcl,lhd->chd/dot_general | solution.py:66
  170.5 0.0 copy-start.7
  170.5 3.0 %fusion.5 = bf16[1536,512]{0,1:T(8,128)(2,1)S(1)} fusion(f32[4,128,1536]{2,1,0:T(8,128)} %get-tuple-element.24, bf16[1536,1024]{0,1:T(8,128)(2,1)} %copy-done.2, f32[512]{0:T(512)S(1)} %bitcast.133, f32[1536]{0:T(1024)S(1)} %add_rsqrt_fusion), kind=kLoop, calls=%fused_computation.20 | loop fusion | flops 3932160 | bytes 6299648 | tf_op jit(solution)/shard_map/convert_element_type | solution.py:131
  173.5 0.3 copy-done.5
  173.8 0.3 copy-done.7
  174.0 2.2 %fusion.13 = bf16[1536,512]{0,1:T(8,128)(2,1)} fusion(f32[1536,512]{0,1:T(8,128)S(1)} %copy-done.5, bf16[1536,512]{0,1:T(8,128)(2,1)S(1)} %fusion.5, bf16[2,512,512]{2,1,0:T(8,128)(2,1)S(1)} %copy-done.7), kind=kOutput, calls=%fused_computation.34 | convolution fusion | flops 806879232 | bytes 6815744 | tf_op jit(solution)/shard_map/dot_general | solution.py:132
  176.2 2.6 %copy.42 = bf16[1536,512]{1,0:T(8,128)(2,1)} copy(bf16[1536,512]{0,1:T(8,128)(2,1)} %fusion.13) | data formatting | bytes 3145728 | tf_op jit(solution)/shard_map/convert_element_type | solution.py:133
  178.8 0.0 copy-done.1
  (31 shorter events, 0.2 us)
Async XLA Ops:
  0.0 1.6 copy-start
  7.0 3.9 %copy-start.8 = (s32[1536,1]{0,1:T(1,128)S(1)}, s32[1536,1]{0,1:T(1,128)}, u32[]{:S(2)}) copy-start(s32[1536,1]{0,1:T(1,128)} %param.15) | copy-start | bytes 18436
  7.0 24.6 %copy-start.14 = (s32[1,8]{1,0:T(1,128)S(1)}, s32[1,8]{1,0:T(1,128)}, u32[]{:S(2)}) copy-start(s32[1,8]{1,0:T(1,128)} %param.14) | copy-start | bytes 100
  7.0 16.4 %all-to-all-start.2 = ((bf16[4,2,2,1,128,512]{5,4,2,0,3,1:T(8,128)(2,1)}), bf16[4,2,2,1,128,512]{5,4,2,0,3,1:T(8,128)(2,1)S(1)}, u32[]{:S(2)}, u32[]{:S(2)}) async-start(bf16[4,2,2,1,128,512]{5,4,2,0,3,1:T(8,128)(2,1)} %copy.35), calls=%async_computation.2 | async-start | bytes 4194304 | tf_op jit(solution)/shard_map/all_to_all | solution.py:32
  23.5 15.8 %all-to-all-start = ((s32[16,1,192]{2,1,0:T(1,128)}), s32[16,1,192]{2,1,0:T(1,128)S(1)}, u32[]{:S(2)}, u32[]{:S(2)}) async-start(s32[16,1,192]{2,1,0:T(1,128)} %all_to_all.19), calls=%async_computation | async-start | bytes 32768 | tf_op jit(solution)/shard_map/all_to_all | solution.py:99
  32.3 11.2 %copy-start.15 = (s32[1,8]{1,0:T(1,128)S(1)}, s32[1,8]{1,0:T(1,128)}, u32[]{:S(2)}) copy-start(s32[1,8]{1,0:T(1,128)} %param.13) | copy-start | bytes 100
  33.9 11.0 %copy-start.10 = (f32[2,512]{1,0:T(2,128)S(1)}, f32[2,512]{1,0:T(2,128)}, u32[]{:S(2)}) copy-start(f32[2,512]{1,0:T(2,128)} %param.17) | copy-start | bytes 12292
  33.9 11.0 %copy-start.11 = (f32[2,512]{1,0:T(2,128)S(1)}, f32[2,512]{1,0:T(2,128)}, u32[]{:S(2)}) copy-start(f32[2,512]{1,0:T(2,128)} %param.20) | copy-start | bytes 12292
  39.2 29.8 %all-to-all-start.3 = ((bf16[4,2,2,1,128,512]{5,4,2,1,3,0:T(8,128)(2,1)}), bf16[4,2,2,1,128,512]{5,4,2,1,3,0:T(8,128)(2,1)S(1)}, u32[]{:S(2)}, u32[]{:S(2)}) async-start(bf16[4,2,2,1,128,512]{5,4,2,1,3,0:T(8,128)(2,1)} %copy.36), calls=%async_computation.3 | async-start | bytes 4194304 | tf_op jit(solution)/shard_map/all_to_all | solution.py:32
  69.0 47.1 %all-to-all-start.1 = ((bf16[16,192,512]{2,1,0:T(8,128)(2,1)}), bf16[16,192,512]{2,1,0:T(8,128)(2,1)}, u32[]{:S(2)}, u32[]{:S(2)}) async-start(bf16[16,192,512]{2,1,0:T(8,128)(2,1)} %broadcast_select_fusion), calls=%async_computation.1 | async-start | bytes 6291456 | tf_op jit(solution)/shard_map/all_to_all | solution.py:101
  74.4 1.6 copy-start.12
  130.2 1.7 copy-start.3
  147.2 3.0 %copy-start.6 = (bf16[2,512,512]{2,1,0:T(8,128)(2,1)S(1)}, bf16[2,512,512]{2,1,0:T(8,128)(2,1)}, u32[]{:S(2)}) copy-start(bf16[2,512,512]{2,1,0:T(8,128)(2,1)} %param.21) | copy-start | bytes 3145732
  150.2 1.6 copy-start.13
  151.4 3.2 %copy-start.4 = (f32[1536,512]{0,1:T(8,128)}, f32[1536,512]{0,1:T(8,128)S(1)}, u32[]{:S(2)}) copy-start(f32[1536,512]{0,1:T(8,128)S(1)} %get-tuple-element.22) | copy-start | bytes 9437188
  154.6 1.7 copy-start.2
  156.4 14.1 %copy-start.9 = (f32[1,512]{1,0:T(1,128)S(1)}, f32[1,512]{1,0:T(1,128)}, u32[]{:S(2)}) copy-start(f32[1,512]{1,0:T(1,128)} %get-tuple-element.15) | copy-start | bytes 6148
  170.4 3.3 %copy-start.5 = (f32[1536,512]{0,1:T(8,128)S(1)}, f32[1536,512]{0,1:T(8,128)}, u32[]{:S(2)}) copy-start(f32[1536,512]{0,1:T(8,128)} %copy-done.4) | copy-start | bytes 9437188
  170.5 3.6 %copy-start.7 = (bf16[2,512,512]{2,1,0:T(8,128)(2,1)S(1)}, bf16[2,512,512]{2,1,0:T(8,128)(2,1)}, u32[]{:S(2)}) copy-start(bf16[2,512,512]{2,1,0:T(8,128)(2,1)} %param.21) | copy-start | bytes 3145732
  174.0 4.8 %copy-start.1 = (bf16[2,8,128,512]{3,2,1,0:T(8,128)(2,1)S(1)}, bf16[2,8,128,512]{3,2,1,0:T(8,128)(2,1)}, u32[]{:S(2)}) copy-start(bf16[2,8,128,512]{3,2,1,0:T(8,128)(2,1)} %param.12) | copy-start | bytes 6291460
where the time goes:
time: 180 us; the launch traced here: 179 us
  local copies, waits for them, and re-layouts  50.4 us (28%)
  waiting for transfers between devices  43.2 us (24%)
  matrix products  42 us (23%)
  other arithmetic  21.9 us (12%)
  starting transfers between devices  21 us (12%)
    all_to_all x1, waiting for transfers between devices, local(): lax.all_to_all(fetched_rows, 'gy', split_axis=0, concat_axis=0, tiled=True)  33.8 us
    dot_general x2, matrix products, attend(): jnp.einsum('hcl,lhd->chd', weights, valued, preferred_element_type=jnp.fl...  28.2 us
    gather x1, local copies, waits for them, and re-layouts, local(): jnp.take(table, lax.all_to_all(requests, 'gy', split_axis=0, concat_axis=...  16 us
    gather x2, local copies, waits for them, and re-layouts, local(): jnp.take(returned.reshape(groups * capacity, feature_count), flat_slot, a...  9.49 us
    all_to_all x2, starting transfers between devices, moved_by_axis(): lax.all_to_all(tiles, axes[k], split_axis=k, concat_axis=k, tiled=True)  8.19 us
    all_to_all x1, starting transfers between devices, local(): lax.all_to_all(requests, 'gy', split_axis=0, concat_axis=0, tiled=True)  8.16 us
    dot_general x2, matrix products, local(): jnp.dot(normed, w_query[layer_index], preferred_element_type=jnp.float32)  6.81 us
    scatter x1, local copies, waits for them, and re-layouts, local(): requests = jnp.zeros((groups * capacity,), jnp.int32).at[flat_slot].set(c...  6.36 us
  transfers between devices with their start and end apart: 4, of which 3 were waited for; matrix products, arithmetic and copies ran while one was open for 24% of the time, Pallas kernels for 0%

commit v1 on v0

v1 whole, which is shorter than its diff:
```python
import functools

import jax
import jax.numpy as jnp
from jax import lax
from jax.experimental import pallas as pl
from jax.experimental.pallas import tpu as pltpu
from jax.sharding import PartitionSpec as P

HEADS = 4
LAYERS = 2
EPSILON = 1e-06
MESH = pl.DeviceIdType.MESH
f32, bf16, i32 = jnp.float32, jnp.bfloat16, jnp.int32

OFFSETS = (
    (2, 2), (1, 0), (2, 1), (0, 3), (1, 2), (3, 0), (2, 3), (0, 1),
    (3, 2), (1, 1), (0, 2), (3, 3), (2, 0), (1, 3), (3, 1),
)
SIDE = 4
PEERS = len(OFFSETS)
PACKED_Z = sum(z * SIDE**k for k, (z, _) in enumerate(OFFSETS))
PACKED_Y = sum(y * SIDE**k for k, (_, y) in enumerate(OFFSETS))


def silu(v):
    half = v * 0.5
    return half + half * jnp.tanh(half)


def rms_scale(vector, gain_row):
    return vector * lax.rsqrt(jnp.mean(vector * vector, axis=-1, keepdims=True) + EPSILON) * gain_row


def bucket_kernel(capacity, owner_ref, row_ref, slot_ref, request_ref, square):
    blocks = owner_ref.shape[0]
    groups = request_ref.shape[0]
    lane = lax.broadcasted_iota(i32, (128, 128), 1)
    below = (lane < lax.broadcasted_iota(i32, (128, 128), 0)).astype(bf16)
    slot_lane = lax.broadcasted_iota(i32, (128, 2 * 128), 1).astype(f32)
    owner_lane = (lane % groups).astype(f32)
    square[...] = jnp.zeros_like(square)
    square[0:blocks, :] = owner_ref[...].astype(f32)
    owners = square[...].T
    square[0:blocks, :] = (row_ref[...] // 64).astype(f32)
    high = square[...].T
    square[0:blocks, :] = (row_ref[...] % 64).astype(f32)
    low = square[...].T
    carry = jnp.zeros((1, 128), f32)
    parts = jnp.zeros((128, 2 * 128), f32)
    for b in range(blocks):
        owner = owners[:, b : b + 1]
        named = owner == owner_lane
        onehot = jnp.where(named & (lane < groups), 1.0, 0.0)
        prior = jnp.dot(below, onehot.astype(bf16), preferred_element_type=f32) + carry
        carry = carry + jnp.sum(onehot, axis=0, keepdims=True)
        rank = jnp.sum(onehot * prior, axis=1, keepdims=True)
        slot_ref[b * 128 : (b + 1) * 128, :] = jnp.broadcast_to(
            owner * capacity + rank, (128, 128)
        ).astype(i32)
        digits = jnp.where(lane < groups, high[:, b : b + 1], low[:, b : b + 1])
        digits = jnp.where(named & (lane < 2 * groups), digits, 0.0)
        chosen = jnp.where(rank == slot_lane, 1.0, 0.0)
        parts = parts + jnp.dot(
            digits.T.astype(bf16), chosen.astype(bf16), preferred_element_type=f32
        )
    rows = (parts[0:groups] * 64.0 + parts[groups : 2 * groups]).astype(i32)
    request_ref[:, 0, :] = rows[:, 0:128]
    request_ref[:, 1, :] = rows[:, 128:256]


def exchange_kernel(
    capacity,
    request_ref,
    slot_ref,
    gain_ref,
    assign_ref,
    length_ref,
    table_hbm,
    history_hbm,
    w_key_hbm,
    stream_ref,
    kv_ref,
    table_in,
    table,
    asked,
    asked_scalar,
    stage,
    outbox,
    inbox,
    total,
    history_in,
    history_out,
    history_all,
    w_key,
    local_sem,
    asked_send,
    asked_recv,
    row_send,
    row_recv,
    hist_send,
    hist_recv,
):
    count = stream_ref.shape[0]
    width = stream_ref.shape[1]
    members = lax.axis_size("gx")
    span = history_in.shape[2]
    gx = lax.axis_index("gx")
    gy = lax.axis_index("gy")
    my_z, my_y = gy // SIDE, gy % SIDE

    def peer(dz, dy):
        return ((my_z + dz + SIDE) % SIDE) * SIDE + (my_y + dy + SIDE) % SIDE

    table_copy = pltpu.make_async_copy(table_hbm, table_in, local_sem.at[0])
    history_copy = pltpu.make_async_copy(history_hbm, history_in, local_sem.at[1])
    weight_copy = pltpu.make_async_copy(w_key_hbm, w_key, local_sem.at[2])
    history_copy.start()
    table_copy.start()
    weight_copy.start()

    barrier = pltpu.get_barrier_semaphore()
    for dz, dy in OFFSETS:
        pl.semaphore_signal(barrier, inc=1, device_id=(gx, peer(dz, dy)), device_id_type=MESH)
    for d in range(1, members):
        pl.semaphore_signal(
            barrier, inc=1, device_id=((gx + d) % members, gy), device_id_type=MESH
        )
    pl.semaphore_wait(barrier, PEERS + members - 1)

    ask = []
    for k, (dz, dy) in enumerate(OFFSETS):
        to = peer(dz, dy)
        ask.append(
            pltpu.make_async_remote_copy(
                request_ref.at[to],
                asked.at[k],
                asked_send.at[k],
                asked_recv.at[k],
                device_id=(gx, to),
                device_id_type=MESH,
            )
        )
        ask[-1].start()

    history_copy.wait()
    for l in range(LAYERS):
        for d in range(1, members):
            to = (gx + d) % members
            history_out[l, d] = history_in[l, assign_ref[0, to]]
        here = pl.ds(pl.multiple_of(gx * span, span), span)
        history_all[l, here, :] = history_in[l, assign_ref[0, gx]]
    spread = []
    for l in range(LAYERS):
        for d in range(1, members):
            to = (gx + d) % members
            spread.append(
                pltpu.make_async_remote_copy(
                    history_out.at[l, d],
                    history_all.at[l, pl.ds(pl.multiple_of(gx * span, span), span), :],
                    hist_send.at[l, d],
                    hist_recv.at[l, d],
                    device_id=(to, gy),
                    device_id_type=MESH,
                )
            )
            spread[-1].start()

    table_copy.wait()
    step = 256

    @pl.loop(0, table_in.shape[0] // step)
    def _(t):
        at = pl.ds(pl.multiple_of(t * step, step), step)
        for c in range(width // 128):
            table[at, c, :] = table_in[at, c * 128 : (c + 1) * 128].astype(f32)

    def collect(index, box, slot):
        @pl.loop(0, capacity // 16)
        def _(t):
            for j in range(16):
                place = t * 16 + j
                row = asked_scalar[index, place // 128, place % 128]
                stage[pl.ds(place, 1)] = table[pl.ds(row, 1)]

        for c in range(width // 128):
            box[slot, :, c * 128 : (c + 1) * 128] = stage[:, c, :].astype(bf16)

    asked[PEERS] = request_ref[gy]
    for k in range(PEERS):
        ask[k].wait_recv()
    scalars = pltpu.make_async_copy(asked, asked_scalar, local_sem.at[3])
    scalars.start()
    scalars.wait()

    def reply(k, dz, dy):
        to = peer(-dz, -dy)
        return pltpu.make_async_remote_copy(
            outbox.at[k],
            inbox.at[k + 1],
            row_send.at[k],
            row_recv.at[k],
            device_id=(gx, to),
            device_id_type=MESH,
        )

    def serve(k, digits):
        z, y, last_z, last_y = digits
        collect(k, outbox, k)

        @pl.when(k > 0)
        def _():
            reply(k - 1, last_z, last_y).start()

        return z // SIDE, y // SIDE, z % SIDE, y % SIDE

    lax.fori_loop(0, PEERS, serve, (PACKED_Z, PACKED_Y, 0, 0))
    reply(PEERS - 1, *OFFSETS[-1]).start()
    collect(PEERS, inbox, 0)

    half = count // 2
    lane = lax.broadcasted_iota(i32, (1, 4 * capacity), 1)

    def place(first):
        target = jnp.zeros((1, 4 * capacity), i32)
        for j in range(4):
            slot = first + j
            if slot == 0:
                owner = gy
            else:
                owner = peer(*OFFSETS[slot - 1])
                reply(slot - 1, *OFFSETS[slot - 1]).wait_recv()
            target = jnp.where(lane // capacity == j, lane - j * capacity + owner * capacity, target)
        rows = inbox[first : first + 4].reshape(4 * capacity, width)

        @pl.loop(0, 2)
        def _(b):
            at = pl.ds(pl.multiple_of(b * half, half), half)
            slots = slot_ref[at, :]
            onehot = jnp.concatenate(
                [
                    jnp.where(slots == target[:, c : c + 128], 1.0, 0.0).astype(bf16)
                    for c in range(0, 4 * capacity, 128)
                ],
                axis=1,
            )
            found = jnp.dot(onehot, rows, preferred_element_type=f32)
            if first == 0:
                total[at, :] = found
            elif first == 12:
                stream_ref[at, :] = (total[at, :] + found).astype(bf16)
            else:
                total[at, :] = total[at, :] + found

    live = length_ref[0, assign_ref[0, gx]]

    def project(l):
        for d in range(1, members):
            spread[l * (members - 1) + d - 1].wait_recv()
        size = 512

        @pl.loop(0, history_all.shape[1] // size)
        def _(b):
            at = pl.ds(pl.multiple_of(b * size, size), size)
            normed = rms_scale(history_all[l, at, :].astype(f32), gain_ref[l : l + 1, :])
            both = silu(jnp.dot(normed.astype(bf16), w_key[l], preferred_element_type=f32))
            position = lax.broadcasted_iota(i32, (size, 1), 0) + b * size
            kv_ref[l, at, 0:width] = both[:, 0:width].astype(bf16)
            kv_ref[l, at, width : 2 * width] = jnp.where(
                position < live, both[:, width : 2 * width], 0.0
            ).astype(bf16)

    weight_copy.wait()
    place(0)
    project(0)
    place(4)
    project(1)
    place(8)
    place(12)
    for k in range(PEERS):
        ask[k].wait_send()
        reply(k, *OFFSETS[k]).wait_send()
    for copy in spread:
        copy.wait_send()


def layers_kernel(emb_ref, kv_ref, wq_ref, wo_ref, gain_ref, attn_ref, out_ref):
    width = emb_ref.shape[1]
    head = width // HEADS
    length = kv_ref.shape[1]
    keys = 256
    stream = emb_ref[...].astype(f32)
    for l in range(LAYERS):
        normed = rms_scale(stream, gain_ref[l : l + 1, :]).astype(bf16)
        gate_query = silu(jnp.dot(normed, wq_ref[l], preferred_element_type=f32)).astype(bf16)
        outs = []
        for h in range(HEADS):
            query = gate_query[:, width + h * head : width + (h + 1) * head]
            total = None
            for k in range(0, length, keys):
                scores = lax.dot_general(
                    query,
                    kv_ref[l, k : k + keys, h * head : (h + 1) * head],
                    (((1,), (1,)), ((), ())),
                    preferred_element_type=f32,
                )
                weights = silu(scores * head**-0.5).astype(bf16)
                part = jnp.dot(
                    weights,
                    kv_ref[l, k : k + keys, width + h * head : width + (h + 1) * head],
                    preferred_element_type=f32,
                )
                total = part if total is None else total + part
            outs.append(total)
        attended = jnp.concatenate(outs, axis=1)
        gated = rms_scale(attended, attn_ref[l : l + 1, :]) * gate_query[:, :width].astype(f32)
        stream = stream + jnp.dot(gated.astype(bf16), wo_ref[l], preferred_element_type=f32)
    out_ref[...] = stream.astype(bf16)


VMEM = pl.BlockSpec(memory_space=pltpu.VMEM)
SMEM = pl.BlockSpec(memory_space=pltpu.SMEM)
ANY = pl.BlockSpec(memory_space=pl.ANY)


def local(
    table,
    history,
    lengths,
    assignment,
    cand_owner,
    cand_row,
    norm_gain,
    w_query,
    w_key,
    attn_gain,
    w_out,
):
    groups = lax.axis_size("gy")
    members = lax.axis_size("gx")
    count = cand_row.shape[0]
    rows, width = table.shape
    span = history.shape[2]
    capacity = 2 * count // groups
    slots, requests = pl.pallas_call(
        functools.partial(bucket_kernel, capacity),
        out_shape=(
            jax.ShapeDtypeStruct((count, 128), i32),
            jax.ShapeDtypeStruct((groups, 2, 128), i32),
        ),
        in_specs=[VMEM, VMEM],
        out_specs=(VMEM, VMEM),
        scratch_shapes=[pltpu.VMEM((128, 128), f32)],
        name="bucket",
    )(cand_owner.reshape(count // 128, 128), cand_row.reshape(count // 128, 128))
    dma = pltpu.SemaphoreType.DMA
    stream, key_value = pl.pallas_call(
        functools.partial(exchange_kernel, capacity),
        out_shape=(
            jax.ShapeDtypeStruct((count, width), bf16),
            jax.ShapeDtypeStruct((LAYERS, span * members, 2 * width), bf16),
        ),
        in_specs=[VMEM, VMEM, VMEM, SMEM, SMEM, ANY, ANY, ANY],
        out_specs=(VMEM, VMEM),
        scratch_shapes=[
            pltpu.VMEM((rows, width), bf16),
            pltpu.VMEM((rows, width // 128, 128), f32),
            pltpu.VMEM((groups, 2, 128), i32),
            pltpu.SMEM((groups, 2, 128), i32),
            pltpu.VMEM((capacity, width // 128, 128), f32),
            pltpu.VMEM((PEERS, capacity, width), bf16),
            pltpu.VMEM((groups, capacity, width), bf16),
            pltpu.VMEM((count, width), f32),
            pltpu.VMEM(history.shape, bf16),
            pltpu.VMEM((LAYERS, members, span, width), bf16),
            pltpu.VMEM((LAYERS, members * span, width), bf16),
            pltpu.VMEM(w_key.shape, bf16),
            dma((4,)),
            dma((PEERS,)),
            dma((PEERS,)),
            dma((PEERS,)),
            dma((PEERS,)),
            dma((LAYERS, members)),
            dma((LAYERS, members)),
        ],
        compiler_params=pltpu.CompilerParams(
            collective_id=0, has_side_effects=True, vmem_limit_bytes=60 << 20
        ),
        name="exchange",
    )(requests, slots, norm_gain, assignment, lengths, table, history, w_key)
    block = count // 2
    return pl.pallas_call(
        layers_kernel,
        grid=(count // block,),
        out_shape=jax.ShapeDtypeStruct((count, width), bf16),
        in_specs=[pl.BlockSpec((block, width), lambda i: (i, 0)), VMEM, VMEM, VMEM, VMEM, VMEM],
        out_specs=pl.BlockSpec((block, width), lambda i: (i, 0)),
        compiler_params=pltpu.CompilerParams(vmem_limit_bytes=60 << 20),
        name="layers",
    )(stream, key_value, w_query, w_out, norm_gain, attn_gain)


def solution(mesh):
    both = ("gx", "gy")
    return jax.shard_map(
        local,
        mesh=mesh,
        in_specs=(
            P("gy", None),
            P(None, "gy", "gx", None),
            P("gy", None),
            P("gy", None),
            P(both, None),
            P(both),
            P(),
            P(),
            P(),
            P(),
            P(),
        ),
        out_specs=P(both, None),
        check_vma=False,
    )
```

time: 180 us -> 94.3 us (0.52)
  Pallas kernels: 0 us -> 92.2 us
  local copies, waits for them, and re-layouts: 50.4 us -> 0 us
  waiting for transfers between devices: 43.2 us -> 0 us
  matrix products: 42 us -> 0 us
  starting transfers between devices: 21 us -> 0 us
  other arithmetic: 21.9 us -> 1.3 us
    pallas_call x0 -> x3, Pallas kernels: none -> 92.2 us  [the longest x1 63.2 us: local(): pl.pallas_call(functools.partial(exchange_kernel, capacity), out_shape=(j...]
    all_to_all x4 -> x0, waiting for transfers between devices: 43.2 us -> none  [the longest x1 33.8 us: local(): lax.all_to_all(fetched_rows, 'gy', split_axis=0, concat_axis=0, tiled=True)]
    dot_general x8 -> x0, matrix products: 42 us -> none  [the longest x2 28.2 us: attend(): jnp.einsum('hcl,lhd->chd', weights, valued, preferred_element_type=jnp.fl...]
    gather x4 -> x0, local copies, waits for them, and re-layouts: 27.6 us -> none  [the longest x1 16 us: local(): jnp.take(table, lax.all_to_all(requests, 'gy', split_axis=0, concat_axis=...]
    all_to_all x4 -> x0, starting transfers between devices: 21 us -> none  [the longest x2 8.19 us: moved_by_axis(): lax.all_to_all(tiles, axes[k], split_axis=k, concat_axis=k, tiled=True)]
    convert_element_type x4 -> x0, other arithmetic: 6.54 us -> none  [the longest x2 5.98 us: local(): gated_out = (rms_scale(attended, attn_gain[layer_index]) * gate_query[:,...]
    scatter x1 -> x0, local copies, waits for them, and re-layouts: 6.36 us -> none  [local(): requests = jnp.zeros((groups * capacity,), jnp.int32).at[flat_slot].set(c...]
    select_n x5 -> x0, other arithmetic: 6.09 us -> none  [the longest x2 3.41 us: local(): jnp.take(table, lax.all_to_all(requests, 'gy', split_axis=0, concat_axis=...]
  transfers between devices with their start and end apart: 4 -> 0, of which waited for: 3 -> 0; matrix products, arithmetic and copies ran while one was open for 24% -> 0% of each run, Pallas kernels for 0% -> 0%
where the time goes in v1:
time: 94.3 us; the launch traced here: 93.5 us
  Pallas kernels  92.2 us (98%)
  other arithmetic  1.3 us (1%)
    pallas_call x1, Pallas kernels, local(): pl.pallas_call(functools.partial(exchange_kernel, capacity), out_shape=(j...  63.2 us
    pallas_call x1, Pallas kernels, local(): pl.pallas_call(layers_kernel, grid=(count // block,), out_shape=jax.Shape...  25.1 us
    pallas_call x1, Pallas kernels, local(): pl.pallas_call(functools.partial(bucket_kernel, capacity), out_shape=(jax...  3.95 us

profile of v1, /device:TPU:0, one launch (start us, length us, event | category | flops | bytes accessed | tf_op | source)
XLA Modules:
  0.0 93.5 jit_solution(10161133045620849989)
XLA Ops:
  0.0 1.3 %reduce = s32[1536]{0:T(1024)} reduce(s32[1536,1]{0,1:T(1,128)} %param.15, s32[]{:T(128)} %constant.3), dimensions={1}, to_apply=%param.15.reduce_sub_computation | reduce | bytes 12292 | tf_op args[4]
  1.3 4.0 %bucket.1 = (s32[1536,128]{1,0:T(8,128)}, s32[16,2,128]{2,1,0:T(2,128)}) custom-call(s32[12,128]{1,0:T(8,128)} %bitcast.2, s32[12,128]{1,0:T(8,128)} %bitcast.3), custom_call_target="tpu_custom_call" | custom-call | tf_op jit(solution)/shard_map/bucket/pallas_call | solution.py:345
  5.3 63.2 %exchange.1 = (bf16[1536,512]{1,0:T(8,128)(2,1)}, bf16[2,1024,1024]{2,1,0:T(8,128)(2,1)}) custom-call(s32[16,2,128]{2,1,0:T(2,128)} %get-tuple-element.9.request_ref, s32[1536,128]{1,0:T(8,128)} %get-tuple-element.10.slot_ref, f32[2,512]{1,0:T(2,128)} %gain_ref.3, s32[1,8]{1,0:T(1,128)} %assign_ref.1, s32[1,8]{1,0:T(1,128)} %length_ref.1, ...), custom_call_target="tpu_custom_call" | custom-call | tf_op jit(solution)/shard_map/exchange/pallas_call | solution.py:357
  68.4 25.1 %layers.1 = bf16[1536,512]{1,0:T(8,128)(2,1)} custom-call(bf16[1536,512]{1,0:T(8,128)(2,1)} %get-tuple-element.11.emb_ref, bf16[2,1024,1024]{2,1,0:T(8,128)(2,1)} %get-tuple-element.12.kv_ref, bf16[2,512,1024]{2,1,0:T(8,128)(2,1)} %wq_ref.1, bf16[2,512,512]{2,1,0:T(8,128)(2,1)} %wo_ref.1, f32[2,512]{1,0:T(2,128)} %gain_ref.3, f32[2,512]{1,0:T(2,128)} %attn_ref.1), custom_call_target="tpu_custom_call" | custom-call | tf_op jit(solution)/shard_map/layers/pallas_call | solution.py:392

commit v2 on v1

v2 whole, which is shorter than its diff:
```python
import functools

import jax
import jax.numpy as jnp
from jax import lax
from jax.experimental import pallas as pl
from jax.experimental.pallas import tpu as pltpu
from jax.sharding import PartitionSpec as P

HEADS = 4
LAYERS = 2
EPSILON = 1e-06
MESH = pl.DeviceIdType.MESH
f32, bf16, i32 = jnp.float32, jnp.bfloat16, jnp.int32

OFFSETS = (
    (2, 2), (1, 0), (2, 1), (0, 3), (1, 2), (3, 0), (2, 3), (0, 1),
    (3, 2), (1, 1), (0, 2), (3, 3), (2, 0), (1, 3), (3, 1),
)
SIDE = 4
PEERS = len(OFFSETS)
PACKED_Z = sum(z * SIDE**k for k, (z, _) in enumerate(OFFSETS))
PACKED_Y = sum(y * SIDE**k for k, (_, y) in enumerate(OFFSETS))


def silu(v):
    half = v * 0.5
    return half + half * jnp.tanh(half)


def rms_scale(vector, gain_row):
    return vector * lax.rsqrt(jnp.mean(vector * vector, axis=-1, keepdims=True) + EPSILON) * gain_row


def program_kernel(
    capacity,
    owner_ref,
    row_ref,
    gain_ref,
    attn_ref,
    assign_ref,
    length_ref,
    table_hbm,
    history_hbm,
    w_key_hbm,
    w_query_hbm,
    w_out_hbm,
    out_ref,
    square,
    counts,
    counts_scalar,
    rank_ref,
    table_in,
    table,
    request,
    asked,
    asked_scalar,
    stage,
    outbox,
    inbox,
    taken,
    total,
    history_in,
    history_out,
    history_all,
    key_value,
    w_key,
    w_query,
    w_out,
    local_sem,
    asked_send,
    asked_recv,
    row_send,
    row_recv,
    hist_send,
    hist_recv,
):
    count, width = out_ref.shape
    half = count // 2
    blocks = count // 128
    groups = lax.axis_size("gy")
    members = lax.axis_size("gx")
    span = history_in.shape[2]
    gx = lax.axis_index("gx")
    gy = lax.axis_index("gy")
    my_z, my_y = gy // SIDE, gy % SIDE

    def peer(dz, dy):
        return ((my_z + dz + SIDE) % SIDE) * SIDE + (my_y + dy + SIDE) % SIDE

    owner_of = [gy] + [peer(dz, dy) for dz, dy in OFFSETS]

    table_copy = pltpu.make_async_copy(table_hbm, table_in, local_sem.at[0])
    history_copy = pltpu.make_async_copy(history_hbm, history_in, local_sem.at[1])
    key_copy = pltpu.make_async_copy(w_key_hbm, w_key, local_sem.at[2])
    query_copy = pltpu.make_async_copy(w_query_hbm, w_query, local_sem.at[3])
    out_copy = pltpu.make_async_copy(w_out_hbm, w_out, local_sem.at[4])
    history_copy.start()
    table_copy.start()
    key_copy.start()
    query_copy.start()
    out_copy.start()

    barrier = pltpu.get_barrier_semaphore()
    for dz, dy in OFFSETS:
        pl.semaphore_signal(barrier, inc=1, device_id=(gx, peer(dz, dy)), device_id_type=MESH)
    for d in range(1, members):
        pl.semaphore_signal(
            barrier, inc=1, device_id=((gx + d) % members, gy), device_id_type=MESH
        )

    lane = lax.broadcasted_iota(i32, (128, 128), 1)
    sublane = lax.broadcasted_iota(i32, (128, 128), 0)
    below = (lane < sublane).astype(bf16)
    slot_lane = lax.broadcasted_iota(i32, (128, 2 * 128), 1).astype(f32)
    owner_lane = (lane % groups).astype(f32)
    square[...] = jnp.zeros_like(square)
    for b in range(blocks):
        square[0, b : b + 1, :] = owner_ref[:, b * 128 : (b + 1) * 128].astype(f32)
    owners = square[0].T
    square[1, 0:blocks, :] = (row_ref[...] // 64).astype(f32)
    high = square[1].T
    square[2, 0:blocks, :] = (row_ref[...] % 64).astype(f32)
    low = square[2].T
    carry = jnp.zeros((1, 128), f32)
    parts = jnp.zeros((128, 2 * 128), f32)
    ranks = []
    for b in range(blocks):
        named = owners[:, b : b + 1] == owner_lane
        onehot = jnp.where(named & (lane < groups), 1.0, 0.0)
        prior = jnp.dot(below, onehot.astype(bf16), preferred_element_type=f32) + carry
        carry = carry + jnp.sum(onehot, axis=0, keepdims=True)
        rank = jnp.sum(onehot * prior, axis=1, keepdims=True)
        ranks.append(rank)
        digits = jnp.where(lane < groups, high[:, b : b + 1], low[:, b : b + 1])
        digits = jnp.where(named & (lane < 2 * groups), digits, 0.0)
        chosen = jnp.where(rank == slot_lane, 1.0, 0.0)
        parts = parts + jnp.dot(
            digits.T.astype(bf16), chosen.astype(bf16), preferred_element_type=f32
        )
    rows = (parts[0:groups] * 64.0 + parts[groups : 2 * groups]).astype(i32)
    rows = jnp.clip(rows, 0, table.shape[0] - 1)
    request[:, 0, :] = rows[:, 0:128]
    request[:, 1, :] = rows[:, 128:256]
    counts[...] = jnp.broadcast_to(carry.astype(i32), counts.shape)

    pl.semaphore_wait(barrier, PEERS + members - 1)

    ask = []
    for k in range(PEERS):
        to = owner_of[k + 1]
        ask.append(
            pltpu.make_async_remote_copy(
                request.at[to],
                asked.at[k],
                asked_send.at[k],
                asked_recv.at[k],
                device_id=(gx, to),
                device_id_type=MESH,
            )
        )
        ask[-1].start()
    count_copy = pltpu.make_async_copy(counts, counts_scalar, local_sem.at[5])
    count_copy.start()

    history_copy.wait()
    for l in range(LAYERS):
        for d in range(1, members):
            to = (gx + d) % members
            history_out[l, d] = history_in[l, assign_ref[0, to]]
        here = pl.ds(pl.multiple_of(gx * span, span), span)
        history_all[l, here, :] = history_in[l, assign_ref[0, gx]]

    spread = []
    for l in range(LAYERS):
        for d in range(1, members):
            to = (gx + d) % members
            spread.append(
                pltpu.make_async_remote_copy(
                    history_out.at[l, d],
                    history_all.at[l, pl.ds(pl.multiple_of(gx * span, span), span), :],
                    hist_send.at[l, d],
                    hist_recv.at[l, d],
                    device_id=(to, gy),
                    device_id_type=MESH,
                )
            )
            spread[-1].start()

    table_copy.wait()
    step = 256

    @pl.loop(0, table_in.shape[0] // step)
    def _(t):
        at = pl.ds(pl.multiple_of(t * step, step), step)
        for c in range(width // 128):
            table[at, c, :] = table_in[at, c * 128 : (c + 1) * 128].astype(f32)

    def collect(index, box, slot):
        for part in range(2):
            @pl.loop(0, min(128, capacity - part * 128) // 16)
            def _(t):
                for j in range(16):
                    row = jnp.clip(asked_scalar[index, part, t * 16 + j], 0, table.shape[0] - 1)
                    stage[pl.ds(part * 128 + t * 16 + j, 1)] = table[pl.ds(row, 1)]

        for c in range(width // 128):
            box[slot, :, c * 128 : (c + 1) * 128] = stage[:, c, :].astype(bf16)

    asked[PEERS] = request[gy]
    for k in range(PEERS):
        ask[k].wait_recv()
    scalars = pltpu.make_async_copy(asked, asked_scalar, local_sem.at[6])
    scalars.start()
    scalars.wait()

    def reply(k, dz, dy):
        to = peer(-dz, -dy)
        return pltpu.make_async_remote_copy(
            outbox.at[k],
            inbox.at[k + 1],
            row_send.at[k],
            row_recv.at[k],
            device_id=(gx, to),
            device_id_type=MESH,
        )

    def serve(k, digits):
        z, y, last_z, last_y = digits
        collect(k, outbox, k)

        @pl.when(k > 0)
        def _():
            reply(k - 1, last_z, last_y).start()

        return z // SIDE, y // SIDE, z % SIDE, y % SIDE

    lax.fori_loop(0, PEERS, serve, (PACKED_Z, PACKED_Y, 0, 0))
    reply(PEERS - 1, *OFFSETS[-1]).start()
    collect(PEERS, inbox, 0)

    order_row = jnp.full((128, 128), groups, i32)
    order_column = jnp.full((128, 128), groups, i32)
    for j in range(groups):
        order_row = jnp.where(lane == owner_of[j], j, order_row)
        order_column = jnp.where(sublane == owner_of[j], j, order_column)
    earlier = ((order_column < order_row) & (sublane < groups)).astype(bf16)
    before = jnp.dot(
        jnp.broadcast_to(carry, (8, 128)).astype(bf16), earlier, preferred_element_type=f32
    )[0:1]
    for b in range(blocks):
        onehot = (owners[:, b : b + 1] == owner_lane) & (lane < groups)
        start = jnp.sum(jnp.where(onehot, before, 0.0), axis=1, keepdims=True)
        rank_ref[b * 128 : (b + 1) * 128, :] = jnp.broadcast_to(ranks[b] + start, (128, 128)).astype(i32)
    count_copy.wait()
    found_counts = [counts_scalar[0, owner_of[j]] for j in range(groups)]
    starts = [jnp.int32(0)]
    for j in range(groups - 1):
        starts.append(starts[-1] + found_counts[j])

    four = 4 * capacity
    four_lane = lax.broadcasted_iota(i32, (1, four), 1)

    def put(first):
        target = jnp.full((1, four), -1, i32)
        for j in range(4):
            slot = first + j
            if slot > 0:
                reply(slot - 1, *OFFSETS[slot - 1]).wait_recv()
            at = four_lane - j * capacity
            target = jnp.where(
                (at >= 0) & (at < found_counts[slot]), at + starts[slot], target
            )
        rows = inbox[first : first + 4].reshape(four, width)
        for b in range(2):
            if (first == 0 and b == 1) or (first == 12 and b == 0):
                continue
            row = lax.broadcasted_iota(i32, (half, 128), 0) + b * half
            onehot = jnp.concatenate(
                [
                    jnp.where(row == target[:, c : c + 128], 1.0, 0.0).astype(bf16)
                    for c in range(0, four, 128)
                ],
                axis=1,
            )
            found = jnp.dot(onehot, rows, preferred_element_type=f32)
            if first == 4 * b:
                taken[b] = found
            else:
                taken[b] = taken[b] + found

    live = length_ref[0, assign_ref[0, gx]]

    def project(l):
        for d in range(1, members):
            spread[l * (members - 1) + d - 1].wait_recv()
        size = 512

        @pl.loop(0, history_all.shape[1] // size)
        def _(b):
            at = pl.ds(pl.multiple_of(b * size, size), size)
            normed = rms_scale(history_all[l, at, :].astype(f32), gain_ref[l : l + 1, :])
            both = silu(jnp.dot(normed.astype(bf16), w_key[l], preferred_element_type=f32))
            position = lax.broadcasted_iota(i32, (size, 1), 0) + b * size
            key_value[l, at, 0:width] = both[:, 0:width].astype(bf16)
            key_value[l, at, width : 2 * width] = jnp.where(
                position < live, both[:, width : 2 * width], 0.0
            ).astype(bf16)

    def score(stream):
        head = width // HEADS
        keys = 256
        for l in range(LAYERS):
            normed = rms_scale(stream, gain_ref[l : l + 1, :]).astype(bf16)
            gate_query = silu(jnp.dot(normed, w_query[l], preferred_element_type=f32)).astype(bf16)
            outs = []
            for h in range(HEADS):
                query = gate_query[:, width + h * head : width + (h + 1) * head]
                attended = None
                for k in range(0, key_value.shape[1], keys):
                    scores = lax.dot_general(
                        query,
                        key_value[l, k : k + keys, h * head : (h + 1) * head],
                        (((1,), (1,)), ((), ())),
                        preferred_element_type=f32,
                    )
                    scores = scores * (0.5 * head**-0.5)
                    weights = (scores + scores * jnp.tanh(scores)).astype(bf16)
                    part = jnp.dot(
                        weights,
                        key_value[l, k : k + keys, width + h * head : width + (h + 1) * head],
                        preferred_element_type=f32,
                    )
                    attended = part if attended is None else attended + part
                outs.append(attended)
            gated = rms_scale(jnp.concatenate(outs, axis=1), attn_ref[l : l + 1, :])
            gated = gated * gate_query[:, :width].astype(f32)
            stream = stream + jnp.dot(gated.astype(bf16), w_out[l], preferred_element_type=f32)
        return stream

    put(0)
    key_copy.wait()
    project(0)
    put(4)
    project(1)
    query_copy.wait()
    out_copy.wait()
    put(8)

    @pl.loop(0, 2)
    def _(b):
        @pl.when(b == 1)
        def _():
            put(12)

        scored = score(taken[b]).astype(bf16)

        @pl.loop(0, 2)
        def _(part):
            at = pl.ds(pl.multiple_of(part * half, half), half)
            rank = rank_ref[at, :]
            onehot = jnp.concatenate(
                [
                    jnp.where(rank == lane[0:1] + (c + b * half), 1.0, 0.0).astype(bf16)
                    for c in range(0, half, 128)
                ],
                axis=1,
            )
            found = jnp.dot(onehot, scored, preferred_element_type=f32)

            @pl.when(b == 0)
            def _():
                total[at, :] = found

            @pl.when(b == 1)
            def _():
                out_ref[at, :] = (total[at, :] + found).astype(bf16)

    for k in range(PEERS):
        ask[k].wait_send()
        reply(k, *OFFSETS[k]).wait_send()
    for copy in spread:
        copy.wait_send()


VMEM = pl.BlockSpec(memory_space=pltpu.VMEM)
SMEM = pl.BlockSpec(memory_space=pltpu.SMEM)
ANY = pl.BlockSpec(memory_space=pl.ANY)


def local(
    table,
    history,
    lengths,
    assignment,
    cand_owner,
    cand_row,
    norm_gain,
    w_query,
    w_key,
    attn_gain,
    w_out,
):
    groups = lax.axis_size("gy")
    members = lax.axis_size("gx")
    count = cand_row.shape[0]
    rows, width = table.shape
    span = history.shape[2]
    capacity = 2 * count // groups
    dma = pltpu.SemaphoreType.DMA
    vmem = pltpu.VMEM
    return pl.pallas_call(
        functools.partial(program_kernel, capacity),
        out_shape=jax.ShapeDtypeStruct((count, width), bf16),
        in_specs=[VMEM, VMEM, VMEM, VMEM, SMEM, SMEM, ANY, ANY, ANY, ANY, ANY],
        out_specs=VMEM,
        scratch_shapes=[
            vmem((3, 128, 128), f32),
            vmem((8, 128), i32),
            pltpu.SMEM((8, 128), i32),
            vmem((count, 128), i32),
            vmem((rows, width), bf16),
            vmem((rows, width // 128, 128), f32),
            vmem((groups, 2, 128), i32),
            vmem((groups, 2, 128), i32),
            pltpu.SMEM((groups, 2, 128), i32),
            vmem((capacity, width // 128, 128), f32),
            vmem((PEERS, capacity, width), bf16),
            vmem((groups, capacity, width), bf16),
            vmem((2, count // 2, width), f32),
            vmem((count, width), f32),
            vmem(history.shape, bf16),
            vmem((LAYERS, members, span, width), bf16),
            vmem((LAYERS, members * span, width), bf16),
            vmem((LAYERS, members * span, 2 * width), bf16),
            vmem(w_key.shape, bf16),
            vmem(w_query.shape, bf16),
            vmem(w_out.shape, bf16),
            dma((7,)),
            dma((PEERS,)),
            dma((PEERS,)),
            dma((PEERS,)),
            dma((PEERS,)),
            dma((LAYERS, members)),
            dma((LAYERS, members)),
        ],
        compiler_params=pltpu.CompilerParams(
            collective_id=0, has_side_effects=True, vmem_limit_bytes=62 << 20
        ),
        name="hstu",
    )(
        cand_owner.T,
        cand_row.reshape(count // 128, 128),
        norm_gain,
        attn_gain,
        assignment,
        lengths,
        table,
        history,
        w_key,
        w_query,
        w_out,
    )


def solution(mesh):
    both = ("gx", "gy")
    return jax.shard_map(
        local,
        mesh=mesh,
        in_specs=(
            P("gy", None),
            P(None, "gy", "gx", None),
            P("gy", None),
            P("gy", None),
            P(both, None),
            P(both),
            P(),
            P(),
            P(),
            P(),
            P(),
        ),
        out_specs=P(both, None),
        check_vma=False,
    )
```

time: 94.3 us -> 81.2 us (0.86)
  the two profiles are of different devices: /device:TPU:0 before, /device:TPU:34 now
where the time goes in v2:
time: 81.2 us; the launch traced here: 81 us
  Pallas kernels  78.4 us (97%)
  local copies, waits for them, and re-layouts  2.65 us (3%)
    pallas_call x1, Pallas kernels, local(): pl.pallas_call(functools.partial(program_kernel, capacity), out_shape=jax...  78.4 us
    unnamed x1, local copies, waits for them, and re-layouts  2.65 us

profile of v2, /device:TPU:34, one launch (start us, length us, event | category | flops | bytes accessed | tf_op | source)
XLA Modules:
  0.0 81.0 jit_solution(5211533073316431568)
XLA Ops:
  0.0 78.4 %hstu.1 = bf16[1536,512]{1,0:T(8,128)(2,1)} custom-call(s32[1,1536]{1,0:T(1,128)} %bitcast.3, s32[12,128]{1,0:T(8,128)} %bitcast.2, f32[2,512]{1,0:T(2,128)} %gain_ref.1, f32[2,512]{1,0:T(2,128)} %attn_ref.1, s32[1,8]{1,0:T(1,128)} %assign_ref.1, s32[1,8]{1,0:T(1,128)} %length_ref.1, bf16[4096,512]{1,0:T(8,128)(2,1)} %table_hbm.1, ...), custom_call_target="tpu_custom_call" | custom-call | tf_op jit(solution)/shard_map/hstu/pallas_call | solution.py:412
  78.4 2.7 %copy.13 = bf16[1536,512]{1,0:T(8,128)(2,1)} copy(bf16[1536,512]{1,0:T(8,128)(2,1)} %hstu.1) | data formatting | bytes 3145728

commit v3 on v2

--- a/solution.py
+++ b/solution.py
@@ -14,8 +14,8 @@
 f32, bf16, i32 = jnp.float32, jnp.bfloat16, jnp.int32
 
 OFFSETS = (
-    (2, 2), (1, 0), (2, 1), (0, 3), (1, 2), (3, 0), (2, 3), (0, 1),
-    (3, 2), (1, 1), (0, 2), (3, 3), (2, 0), (1, 3), (3, 1),
+    (0, 1), (1, 0), (0, 3), (3, 0), (1, 1), (3, 3), (1, 3), (3, 1),
+    (0, 2), (2, 0), (2, 1), (1, 2), (2, 3), (3, 2), (2, 2),
 )
 SIDE = 4
 PEERS = len(OFFSETS)
@@ -193,8 +193,7 @@
     @pl.loop(0, table_in.shape[0] // step)
     def _(t):
         at = pl.ds(pl.multiple_of(t * step, step), step)
-        for c in range(width // 128):
-            table[at, c, :] = table_in[at, c * 128 : (c + 1) * 128].astype(f32)
+        table[at, :] = table_in[at, :].astype(f32)
 
     def collect(index, box, slot):
         for part in range(2):
@@ -202,10 +201,9 @@
             def _(t):
                 for j in range(16):
                     row = jnp.clip(asked_scalar[index, part, t * 16 + j], 0, table.shape[0] - 1)
-                    stage[pl.ds(part * 128 + t * 16 + j, 1)] = table[pl.ds(row, 1)]
-
-        for c in range(width // 128):
-            box[slot, :, c * 128 : (c + 1) * 128] = stage[:, c, :].astype(bf16)
+                    stage[pl.ds(part * 128 + t * 16 + j, 1), :] = table[pl.ds(row, 1), :]
+
+        box[slot] = stage[...].astype(bf16)
 
     asked[PEERS] = request[gy]
     for k in range(PEERS):
@@ -420,11 +418,11 @@
             pltpu.SMEM((8, 128), i32),
             vmem((count, 128), i32),
             vmem((rows, width), bf16),
-            vmem((rows, width // 128, 128), f32),
+            vmem((rows, width), f32),
             vmem((groups, 2, 128), i32),
             vmem((groups, 2, 128), i32),
             pltpu.SMEM((groups, 2, 128), i32),
-            vmem((capacity, width // 128, 128), f32),
+            vmem((capacity, width), f32),
             vmem((PEERS, capacity, width), bf16),
             vmem((groups, capacity, width), bf16),
             vmem((2, count // 2, width), f32),

time: 81.2 us -> 79.8 us (0.983)
  the two profiles are of different devices: /device:TPU:34 before, /device:TPU:0 now
where the time goes in v3:
time: 79.8 us; the launch traced here: 79.3 us
  Pallas kernels  76.7 us (96%)
  local copies, waits for them, and re-layouts  2.65 us (3%)
    pallas_call x1, Pallas kernels, local(): pl.pallas_call(functools.partial(program_kernel, capacity), out_shape=jax...  76.7 us
    unnamed x1, local copies, waits for them, and re-layouts  2.65 us

profile of v3, /device:TPU:0, one launch (start us, length us, event | category | flops | bytes accessed | tf_op | source)
XLA Modules:
  0.0 79.3 jit_solution(19637622091805491)
XLA Ops:
  0.0 76.7 %hstu.1 = bf16[1536,512]{1,0:T(8,128)(2,1)} custom-call(s32[1,1536]{1,0:T(1,128)} %bitcast.3, s32[12,128]{1,0:T(8,128)} %bitcast.2, f32[2,512]{1,0:T(2,128)} %gain_ref.1, f32[2,512]{1,0:T(2,128)} %attn_ref.1, s32[1,8]{1,0:T(1,128)} %assign_ref.1, s32[1,8]{1,0:T(1,128)} %length_ref.1, bf16[4096,512]{1,0:T(8,128)(2,1)} %table_hbm.1, ...), custom_call_target="tpu_custom_call" | custom-call | tf_op jit(solution)/shard_map/hstu/pallas_call | solution.py:410
  76.7 2.7 %copy.13 = bf16[1536,512]{1,0:T(8,128)(2,1)} copy(bf16[1536,512]{1,0:T(8,128)(2,1)} %hstu.1) | data formatting | bytes 3145728
